TPU v7x, 256 devices: a whole 4x4x8 slice. The times are simulated.
256 devices in a mesh: lon: 32 (over y, z), lat: 8 (over x, core).
Axes of the slice: x: 4, y: 4, z: 8, core: 2. Of those that a mesh axis runs over, the one named last changes fastest.
Arguments:
- height: float32 [1024, 512, 1024], P(None, 'lon', 'lat'), may hold values from -1 to 1
- land_sea: int32 [512, 1024], P('lon', 'lat'), may hold values 0 or 1
- patterns: bfloat16 [512, 2, 512, 1024], P(None, None, 'lon', 'lat'), may hold values from -0.01171875 to 0.01171875
Outputs:
- covariance: float32 [32, 512, 512], P('lon', 'lat')
All inputs are finite; a program needn't handle non-finite values. No bound on the sum of `land_sea` on one device may be relied on, other than what follows from the above.
Results may differ from a plain program's by a relative error of at most 0.0003.
The roundings to bfloat16 on the way count: a program that leaves them out, or rounds other values in their place, can miss the bound.
Values sent between devices are 32-bit elements; how exact they have to be, the bound alone decides.
A program may use at most 128 MiB of HBM per device.

v0:
```python
import math
import jax
import jax.numpy as jnp
from jax import lax
from jax.sharding import PartitionSpec as P

LAG_DEV = 1
GRAVITY = 9.81
ROTATION = 7.2921e-05
EARTH_RADIUS = 6371000.0
LAT_SOUTH = 20.0
LAT_SPAN = 45.0
LON_STEP = 1.0 / 12.0


def padded_2(shard, sides, width):
    for axis, dim in sides:
        devices, length = (lax.axis_size(axis), shard.shape[dim])
        up = [(i, (i + 1) % devices) for i in range(devices - 1)]
        down = [(j, i) for i, j in up]
        last = lax.slice_in_dim(shard, length - width, length, axis=dim)
        initial = lax.slice_in_dim(shard, 0, width, axis=dim)
        before = lax.ppermute(last, axis, up)
        after = lax.ppermute(initial, axis, down)
        shard = jnp.concatenate([before, shard, after], axis=dim)
    return shard


def stencil_coefs(rows_index, total_rows):
    degrees = LAT_SOUTH + LAT_SPAN * (rows_index.astype(jnp.float32) + 0.5) / total_rows
    radians = degrees * (math.pi / 180.0)
    coriolis = 2.0 * ROTATION * jnp.sin(radians)
    north_step = EARTH_RADIUS * (LAT_SPAN / total_rows) * (math.pi / 180.0)
    east_step = EARTH_RADIUS * jnp.cos(radians) * (LON_STEP * math.pi / 180.0)
    return (-GRAVITY / (coriolis * 2.0 * north_step), GRAVITY / (coriolis * 2.0 * east_step))


def velocities(padded, coef_east, coef_north, ocean):
    lat_diff = padded[:, 1:-1, 2:] - padded[:, 1:-1, :-2]
    lon_diff = padded[:, 2:, 1:-1] - padded[:, :-2, 1:-1]
    return (coef_east * lat_diff * ocean, coef_north * lon_diff * ocean)


def on_device(height, land_sea, patterns):
    days, lon_cells, lat_cells = height.shape
    lat_devices = lax.axis_size("lat")
    lon_devices = lax.axis_size("lon")
    total_rows = lat_cells * lat_devices
    lat_place = lax.axis_index("lat")
    lon_place = lax.axis_index("lon")
    rows_index = lat_place * lat_cells + jnp.arange(lat_cells, dtype=jnp.int32)
    coef_east, coef_north = stencil_coefs(rows_index, total_rows)
    ocean = land_sea.astype(jnp.float32)
    padded = padded_2(height, (("lon", 1), ("lat", 2)), 1)
    east_vel, north_vel = velocities(padded, coef_east, coef_north, ocean)
    local_energy = jnp.sum(east_vel * east_vel + north_vel * north_vel)
    stacked = (
        jnp.stack([east_vel, north_vel], axis=1)
        .astype(jnp.bfloat16)
        .reshape(days, 2 * lon_cells * lat_cells)
    )
    mode_count = patterns.shape[0]
    owned = mode_count // lat_devices
    flat_patterns = patterns.reshape(mode_count, 2 * lon_cells * lat_cells)
    energy = lax.psum(local_energy, ("lon", "lat"))
    totals = lax.psum(
        lax.dot_general(
            flat_patterns, stacked, (((1,), (1,)), ((), ())), preferred_element_type=jnp.float32
        ),
        ("lon", "lat"),
    )
    cell_total = 2.0 * days * lon_cells * lon_devices * total_rows
    centered = totals - jnp.mean(totals, axis=1, keepdims=True)
    normed = centered / jnp.sqrt(energy / cell_total + 1e-06)
    my_rows = lax.dynamic_slice_in_dim(normed, lat_place * owned, owned, 0)
    padded_rows = jnp.concatenate([my_rows, jnp.zeros_like(my_rows)], axis=1)
    lag = lon_place * LAG_DEV + 0
    shifted = lax.dynamic_slice_in_dim(padded_rows, lag, days, 1)
    product = lax.dot_general(
        shifted,
        normed,
        (((1,), (1,)), ((), ())),
        precision=lax.Precision.HIGHEST,
        preferred_element_type=jnp.float32,
    )
    results = [product / (days - lag).astype(jnp.float32)]
    return jnp.stack(results, axis=0)


def solution(mesh):
    placed = (P(None, "lon", "lat"), P("lon", "lat"), P(None, None, "lon", "lat"))
    return jax.shard_map(
        on_device, mesh=mesh, in_specs=placed, out_specs=P("lon", "lat", None), check_vma=False
    )
```

profile of v0, /device:TPU:2, one launch (start us, length us, event | category | flops | bytes accessed | tf_op | source)
XLA Modules:
  0.0 381.3 jit_solution(7635947852473987990)
XLA Ops:
  6.5 0.0 all-reduce.3.cloned.1.call-start
  6.5 6.1 %copy.10 = f32[1024,16,128]{2,0,1:T(8,128)S(1)} copy(f32[1024,16,128]{2,1,0:T(8,128)} %param.3) | data formatting | bytes 16777216 | tf_op args[0]
  12.6 0.0 copy-start.1
  12.6 3.3 copy-done.1
  15.9 0.1 fusion.23
  16.0 3.9 %collective-permute-start = (f32[1024,1,128]{2,0,1:T(8,128)S(1)}, f32[1024,1,128]{2,0,1:T(8,128)S(1)}, u32[]{:S(2)}, u32[]{:S(2)}) collective-permute-start(f32[1024,1,128]{2,0,1:T(8,128)S(1)} %get-tuple-element.11), channel_id=1, source_target_pairs={{0,8},{8,16},{16,24},{24,32},{32,40},{40,48},{48,56},{56,64},{64,7... | collective-permute-start | bytes 1572872 | tf_op jit(solution)/shard_map/ppermute | solution.py:23
  19.9 1.3 collective-permute-start.1
  21.2 0.0 copy-done.2
  21.2 9.8 %collective-permute-done = f32[1024,1,128]{2,0,1:T(8,128)S(1)} collective-permute-done((f32[1024,1,128]{2,0,1:T(8,128)S(1)}, f32[1024,1,128]{2,0,1:T(8,128)S(1)}, u32[]{:S(2)}, u32[]{:S(2)}) %collective-permute-start) | collective-permute-done | bytes 524320 | tf_op jit(solution)/shard_map/ppermute | solution.py:23
  31.0 5.8 %constant_dynamic-update-slice_fusion.1 = f32[1024,18,128]{2,0,1:T(8,128)S(1)} fusion(f32[1024,18,128]{2,0,1:T(8,128)S(1)} %constant_dynamic-update-slice_fusion.2, f32[1024,16,128]{2,1,0:T(8,128)} %param.3), kind=kLoop, calls=%fused_computation.24 | loop fusion | bytes 16777216
  36.8 0.0 collective-permute-done.1
  36.9 0.0 copy-start
  36.9 8.4 %fusion.22 = (f32[1024,18,1]{2,0,1:T(8,128)}, f32[1024,18,1]{2,0,1:T(8,128)}) fusion(f32[1024,18,128]{2,0,1:T(8,128)S(1)} %constant_dynamic-update-slice_fusion), kind=kLoop, calls=%fused_computation.35 | loop fusion | bytes 294912 | tf_op jit(solution)/shard_map/slice | solution.py:22
  45.3 0.9 copy-done
  46.2 5.6 %copy.13 = f32[1024,18,1]{0,2,1:T(1,128)S(1)} copy(f32[1024,18,1]{2,0,1:T(8,128)} %get-tuple-element.8) | data formatting | bytes 147456 | tf_op jit(solution)/shard_map/slice | solution.py:22
  51.8 1.9 collective-permute-start.2
  53.7 5.6 %copy.15 = f32[1024,18,1]{0,2,1:T(1,128)S(1)} copy(f32[1024,18,1]{2,0,1:T(8,128)} %get-tuple-element.9) | data formatting | bytes 147456 | tf_op jit(solution)/shard_map/slice | solution.py:21
  59.3 2.6 collective-permute-start.3
  61.9 0.1 multiply_divide_fusion
  62.0 0.0 collective-permute-done.2
  62.0 5.1 %copy.14 = f32[1024,18,1]{2,0,1:T(8,128)} copy(f32[1024,18,1]{0,2,1:T(1,128)S(1)} %collective-permute-done.2) | data formatting | bytes 147456 | tf_op jit(solution)/shard_map/ppermute | solution.py:24
  67.1 0.0 collective-permute-done.3
  67.1 5.2 %copy.16 = f32[1024,18,1]{2,0,1:T(8,128)} copy(f32[1024,18,1]{0,2,1:T(1,128)S(1)} %collective-permute-done.3) | data formatting | bytes 147456 | tf_op jit(solution)/shard_map/ppermute | solution.py:23
  72.2 18.3 %add_reduce_fusion = (f32[]{:T(128)}, bf16[1024,16,128]{2,0,1:T(8,128)(2,1)S(1)}, bf16[1024,1,16,128]{3,0,2,1:T(8,128)(2,1)S(1)}) fusion(f32[16,128]{1,0:T(8,128)S(1)} %convert_element_type.18, f32[1024,16,128]{2,0,1:T(8,128)} %copy-done.1, f32[1024,1,128]{2,0,1:T(8,128)S(1)} %collective-permute-done, f32[1024,1,128]{2,0,1:T(8,128)S(1)} %collective-permute-done.1, ...), kind=kLoop, calls=%fused_computation.14 | loop fusion | flops 33554432 | bytes 27419652 | tf_op jit(solution)/shard_map/reduce_sum | solution.py:56
  90.5 8.1 %fusion.11 = f32[512,1024]{0,1:T(8,128)} fusion(bf16[512,2,16,128]{3,2,1,0:T(8,128)(2,1)} %param.5, bf16[1024,1,16,128]{3,0,2,1:T(8,128)(2,1)S(1)} %get-tuple-element.7, bf16[1024,1,16,128]{3,0,2,1:T(8,128)(2,1)S(1)} %bitcast.14), kind=kOutput, calls=%fused_computation.19 | convolution fusion | flops 4299161600 | bytes 14680064 | tf_op jit(solution)/shard_map/dot_general | solution.py:67
  98.6 0.0 all-reduce.3.cloned.1.call-update
  98.7 80.3 %psum.15 = f32[]{:T(128)} all-reduce(f32[]{:T(128)} %get-tuple-element.5), channel_id=1, replica_groups=mesh['lon'=32,'lat'=8] {'lon','lat'}, use_global_device_ids=true, to_apply=%region_3.0 | all-reduce | flops 1 | bytes 8 | tf_op jit(solution)/shard_map/psum | solution.py:65
  179.7 188.9 %all-reduce.3.cloned.1.call-done = f32[512,1024]{0,1:T(8,128)} async-done(((f32[512,1024]{0,1:T(8,128)}), f32[512,1024]{0,1:T(8,128)}) %all-reduce.3.cloned.1.call-update) | async-done | bytes 2097168 | tf_op jit(solution)/shard_map/psum | solution.py:66
  368.6 1.8 reduce_sum.18
  370.4 1.9 subtract_divide_fusion
  372.2 0.2 constant_dynamic-slice_fusion
  372.4 2.0 fusion.16
  (5 shorter events, 0.1 us)
Async XLA Ops:
  6.5 14.6 %copy-start.2 = (s32[16,128]{1,0:T(8,128)S(1)}, s32[16,128]{1,0:T(8,128)}, u32[]{:S(2)}) copy-start(s32[16,128]{1,0:T(8,128)} %param.4) | copy-start | bytes 24580
  6.5 362.0 %all-reduce.3.cloned.1.call-start = ((), (), s32[]{:S(2)}) async-start(), calls=%async_computation | async-start | bytes 4194304 | tf_op jit(solution)/shard_map/psum | solution.py:66
  12.6 3.3 copy-start.1
  16.0 15.0 %collective-permute-start = (f32[1024,1,128]{2,0,1:T(8,128)S(1)}, f32[1024,1,128]{2,0,1:T(8,128)S(1)}, u32[]{:S(2)}, u32[]{:S(2)}) collective-permute-start(f32[1024,1,128]{2,0,1:T(8,128)S(1)} %get-tuple-element.11), channel_id=1, source_target_pairs={{0,8},{8,16},{16,24},{24,32},{32,40},{40,48},{48,56},{56,64},{64,7... | collective-permute-start | bytes 1572872 | tf_op jit(solution)/shard_map/ppermute | solution.py:23
  19.9 17.0 %collective-permute-start.1 = (f32[1024,1,128]{2,0,1:T(8,128)S(1)}, f32[1024,1,128]{2,0,1:T(8,128)S(1)}, u32[]{:S(2)}, u32[]{:S(2)}) collective-permute-start(f32[1024,1,128]{2,0,1:T(8,128)S(1)} %get-tuple-element.10), channel_id=1, source_target_pairs={{8,0},{16,8},{24,16},{32,24},{40,32},{48,40},{56,48},{64,56},{72,6... | collective-permute-start | bytes 1572872 | tf_op jit(solution)/shard_map/ppermute | solution.py:24
  36.9 9.3 %copy-start = (f32[1024,18,128]{2,0,1:T(8,128)}, f32[1024,18,128]{2,0,1:T(8,128)S(1)}, u32[]{:S(2)}) copy-start(f32[1024,18,128]{2,0,1:T(8,128)S(1)} %constant_dynamic-update-slice_fusion) | copy-start | bytes 28311556
  51.8 10.2 %collective-permute-start.2 = (f32[1024,18,1]{0,2,1:T(1,128)S(1)}, f32[1024,18,1]{0,2,1:T(1,128)S(1)}, u32[]{:S(2)}, u32[]{:S(2)}) collective-permute-start(f32[1024,18,1]{0,2,1:T(1,128)S(1)} %copy.13), channel_id=1, source_target_pairs={{1,0},{2,1},{3,2},{4,3},{5,4},{6,5},{7,6},{9,8},{10,9},{11,10},{12... | collective-permute-start | bytes 221192 | tf_op jit(solution)/shard_map/ppermute | solution.py:24
  59.3 7.8 %collective-permute-start.3 = (f32[1024,18,1]{0,2,1:T(1,128)S(1)}, f32[1024,18,1]{0,2,1:T(1,128)S(1)}, u32[]{:S(2)}, u32[]{:S(2)}) collective-permute-start(f32[1024,18,1]{0,2,1:T(1,128)S(1)} %copy.15), channel_id=1, source_target_pairs={{0,1},{1,2},{2,3},{3,4},{4,5},{5,6},{6,7},{8,9},{9,10},{10,11},{11... | collective-permute-start | bytes 221192 | tf_op jit(solution)/shard_map/ppermute | solution.py:23
Sparse Core Ops, SparseCore 0:
  98.8 269.7 all-reduce.2
where the time goes:
time: 382 us; the launch traced here: 381 us
  waiting for transfers between devices  199 us (52%)
  blocking collectives  80.3 us (21%)
  local copies, waits for them, and re-layouts  46.3 us (12%)
  other arithmetic  22 us (6%)
  between operations  14.2 us (4%)
  matrix products  10.1 us (3%)
  starting transfers between devices  9.66 us (3%)
    psum x1, waiting for transfers between devices, on_device(): lax.psum(lax.dot_general(flat_patterns, stacked, (((1,), (1,)), ((), ()))...  189 us
    psum x1, blocking collectives, on_device(): energy = lax.psum(local_energy, ('lon', 'lat'))  80.3 us
    reduce_sum x1, other arithmetic, on_device(): local_energy = jnp.sum(east_vel * east_vel + north_vel * north_vel)  18.3 us
    unnamed x9, local copies, waits for them, and re-layouts  16.1 us
    slice x3, local copies, waits for them, and re-layouts, padded_2(): initial = lax.slice_in_dim(shard, 0, width, axis=dim)  14.1 us
    ppermute x2, waiting for transfers between devices, padded_2(): before = lax.ppermute(last, axis, up)  9.8 us
    dot_general x1, matrix products, on_device(): lax.dot_general(flat_patterns, stacked, (((1,), (1,)), ((), ())), preferr...  8.1 us
  transfers between devices with their start and end apart: 5, of which 2 were waited for; matrix products, arithmetic and copies ran while one was open for 4% of the time, Pallas kernels for 0%

commit v1 on v0

--- a/solution.py
+++ b/solution.py
@@ -63,12 +63,11 @@
     owned = mode_count // lat_devices
     flat_patterns = patterns.reshape(mode_count, 2 * lon_cells * lat_cells)
     energy = lax.psum(local_energy, ("lon", "lat"))
-    totals = lax.psum(
-        lax.dot_general(
-            flat_patterns, stacked, (((1,), (1,)), ((), ())), preferred_element_type=jnp.float32
-        ),
-        ("lon", "lat"),
+    totals = lax.dot_general(
+        flat_patterns, stacked, (((1,), (1,)), ((), ())), preferred_element_type=jnp.float32
     )
+    for mesh_axis in ("lat", "lon"):
+        totals = lax.psum(totals, mesh_axis)
     cell_total = 2.0 * days * lon_cells * lon_devices * total_rows
     centered = totals - jnp.mean(totals, axis=1, keepdims=True)
     normed = centered / jnp.sqrt(energy / cell_total + 1e-06)

time: 382 us -> 346 us (0.906)
  waiting for transfers between devices: 199 us -> 165 us
    psum x1 -> x2, waiting for transfers between devices: 189 us -> 155 us  [on_device(): totals = lax.psum(totals, mesh_axis)]
  transfers between devices with their start and end apart: 5 -> 6, of which waited for: 2 -> 3; matrix products, arithmetic and copies ran while one was open for 4% -> 5% of each run, Pallas kernels for 0% -> 0%
where the time goes in v1:
time: 346 us; the launch traced here: 345 us
  waiting for transfers between devices  165 us (48%)
  blocking collectives  78.2 us (23%)
  local copies, waits for them, and re-layouts  46.3 us (13%)
  other arithmetic  22 us (6%)
  between operations  14.2 us (4%)
  matrix products  10.1 us (3%)
  starting transfers between devices  9.7 us (3%)
    psum x2, waiting for transfers between devices, on_device(): totals = lax.psum(totals, mesh_axis)  155 us
    psum x1, blocking collectives, on_device(): energy = lax.psum(local_energy, ('lon', 'lat'))  78.2 us
    reduce_sum x1, other arithmetic, on_device(): local_energy = jnp.sum(east_vel * east_vel + north_vel * north_vel)  18.3 us
    unnamed x9, local copies, waits for them, and re-layouts  16.1 us
    slice x3, local copies, waits for them, and re-layouts, padded_2(): initial = lax.slice_in_dim(shard, 0, width, axis=dim)  14.1 us
    ppermute x2, waiting for transfers between devices, padded_2(): before = lax.ppermute(last, axis, up)  9.8 us
    dot_general x1, matrix products, on_device(): lax.dot_general(flat_patterns, stacked, (((1,), (1,)), ((), ())), preferr...  8.1 us
  transfers between devices with their start and end apart: 6, of which 3 were waited for; matrix products, arithmetic and copies ran while one was open for 5% of the time, Pallas kernels for 0%

profile of v1, /device:TPU:2, one launch (start us, length us, event | category | flops | bytes accessed | tf_op | source)
XLA Modules:
  0.0 345.5 jit_solution(9447380424828231364)
XLA Ops:
  6.5 6.1 %copy.10 = f32[1024,16,128]{2,0,1:T(8,128)S(1)} copy(f32[1024,16,128]{2,1,0:T(8,128)} %param.3) | data formatting | bytes 16777216 | tf_op args[0]
  12.6 0.0 copy-start.1
  12.6 3.3 copy-done.1
  15.9 0.1 fusion.23
  16.0 3.9 %collective-permute-start = (f32[1024,1,128]{2,0,1:T(8,128)S(1)}, f32[1024,1,128]{2,0,1:T(8,128)S(1)}, u32[]{:S(2)}, u32[]{:S(2)}) collective-permute-start(f32[1024,1,128]{2,0,1:T(8,128)S(1)} %get-tuple-element.11), channel_id=1, source_target_pairs={{0,8},{8,16},{16,24},{24,32},{32,40},{40,48},{48,56},{56,64},{64,7... | collective-permute-start | bytes 1572872 | tf_op jit(solution)/shard_map/ppermute | solution.py:23
  19.9 1.3 collective-permute-start.1
  21.2 9.8 %collective-permute-done = f32[1024,1,128]{2,0,1:T(8,128)S(1)} collective-permute-done((f32[1024,1,128]{2,0,1:T(8,128)S(1)}, f32[1024,1,128]{2,0,1:T(8,128)S(1)}, u32[]{:S(2)}, u32[]{:S(2)}) %collective-permute-start) | collective-permute-done | bytes 524320 | tf_op jit(solution)/shard_map/ppermute | solution.py:23
  31.0 5.8 %constant_dynamic-update-slice_fusion.1 = f32[1024,18,128]{2,0,1:T(8,128)S(1)} fusion(f32[1024,18,128]{2,0,1:T(8,128)S(1)} %constant_dynamic-update-slice_fusion.2, f32[1024,16,128]{2,1,0:T(8,128)} %param.3), kind=kLoop, calls=%fused_computation.24 | loop fusion | bytes 16777216
  36.8 0.0 collective-permute-done.1
  36.9 8.4 %fusion.22 = (f32[1024,18,1]{2,0,1:T(8,128)}, f32[1024,18,1]{2,0,1:T(8,128)}) fusion(f32[1024,18,128]{2,0,1:T(8,128)S(1)} %constant_dynamic-update-slice_fusion), kind=kLoop, calls=%fused_computation.35 | loop fusion | bytes 294912 | tf_op jit(solution)/shard_map/slice | solution.py:22
  45.3 0.9 copy-done
  46.2 5.6 %copy.13 = f32[1024,18,1]{0,2,1:T(1,128)S(1)} copy(f32[1024,18,1]{2,0,1:T(8,128)} %get-tuple-element.8) | data formatting | bytes 147456 | tf_op jit(solution)/shard_map/slice | solution.py:22
  51.8 1.9 collective-permute-start.2
  53.7 5.6 %copy.15 = f32[1024,18,1]{0,2,1:T(1,128)S(1)} copy(f32[1024,18,1]{2,0,1:T(8,128)} %get-tuple-element.9) | data formatting | bytes 147456 | tf_op jit(solution)/shard_map/slice | solution.py:21
  59.3 2.6 collective-permute-start.3
  61.9 0.1 multiply_divide_fusion
  62.0 0.0 collective-permute-done.2
  62.0 5.1 %copy.14 = f32[1024,18,1]{2,0,1:T(8,128)} copy(f32[1024,18,1]{0,2,1:T(1,128)S(1)} %collective-permute-done.2) | data formatting | bytes 147456 | tf_op jit(solution)/shard_map/ppermute | solution.py:24
  67.1 0.0 collective-permute-done.3
  67.1 5.2 %copy.16 = f32[1024,18,1]{2,0,1:T(8,128)} copy(f32[1024,18,1]{0,2,1:T(1,128)S(1)} %collective-permute-done.3) | data formatting | bytes 147456 | tf_op jit(solution)/shard_map/ppermute | solution.py:23
  72.2 18.3 %add_reduce_fusion = (f32[]{:T(128)}, bf16[1024,16,128]{2,0,1:T(8,128)(2,1)S(1)}, bf16[1024,1,16,128]{3,0,2,1:T(8,128)(2,1)S(1)}) fusion(f32[16,128]{1,0:T(8,128)S(1)} %convert_element_type.18, f32[1024,16,128]{2,0,1:T(8,128)} %copy-done.1, f32[1024,1,128]{2,0,1:T(8,128)S(1)} %collective-permute-done, f32[1024,1,128]{2,0,1:T(8,128)S(1)} %collective-permute-done.1, ...), kind=kLoop, calls=%fused_computation.14 | loop fusion | flops 33554432 | bytes 27419652 | tf_op jit(solution)/shard_map/reduce_sum | solution.py:56
  90.5 8.1 %fusion.11 = f32[512,1024]{0,1:T(8,128)} fusion(bf16[512,2,16,128]{3,2,1,0:T(8,128)(2,1)} %param.5, bf16[1024,1,16,128]{3,0,2,1:T(8,128)(2,1)S(1)} %get-tuple-element.7, bf16[1024,1,16,128]{3,0,2,1:T(8,128)(2,1)S(1)} %bitcast.14), kind=kOutput, calls=%fused_computation.19 | convolution fusion | flops 4299161600 | bytes 14680064 | tf_op jit(solution)/shard_map/dot_general | solution.py:66
  98.6 0.0 all-reduce.4.cloned.1.call-update
  98.7 0.0 all-reduce.6.cloned.1.call-start
  98.7 73.7 %all-reduce.4.cloned.1.call-done = f32[512,1024]{0,1:T(8,128)} async-done(((f32[512,1024]{0,1:T(8,128)}), f32[512,1024]{0,1:T(8,128)}) %all-reduce.4.cloned.1.call-update) | async-done | bytes 2097168 | tf_op jit(solution)/shard_map/psum | solution.py:70
  172.5 0.0 all-reduce.6.cloned.1.call-update
  172.5 78.2 %psum.23 = f32[]{:T(128)} all-reduce(f32[]{:T(128)} %get-tuple-element.5), channel_id=1, replica_groups=mesh['lon'=32,'lat'=8] {'lon','lat'}, use_global_device_ids=true, to_apply=%region_4.0 | all-reduce | flops 1 | bytes 8 | tf_op jit(solution)/shard_map/psum | solution.py:65
  251.4 81.4 %all-reduce.6.cloned.1.call-done = f32[512,1024]{0,1:T(8,128)} async-done(((f32[512,1024]{0,1:T(8,128)}), f32[512,1024]{0,1:T(8,128)}) %all-reduce.6.cloned.1.call-update) | async-done | bytes 2097168 | tf_op jit(solution)/shard_map/psum | solution.py:70
  332.7 1.8 reduce_sum.18
  334.5 1.9 subtract_divide_fusion
  336.4 0.2 constant_dynamic-slice_fusion
  336.6 2.0 fusion.16
  (8 shorter events, 0.1 us)
Async XLA Ops:
  6.5 14.6 %copy-start.2 = (s32[16,128]{1,0:T(8,128)S(1)}, s32[16,128]{1,0:T(8,128)}, u32[]{:S(2)}) copy-start(s32[16,128]{1,0:T(8,128)} %param.4) | copy-start | bytes 24580
  6.5 165.9 %all-reduce.4.cloned.1.call-start = ((), (), s32[]{:S(2)}) async-start(), calls=%async_computation | async-start | bytes 4194304 | tf_op jit(solution)/shard_map/psum | solution.py:70
  12.6 3.3 copy-start.1
  16.0 15.0 %collective-permute-start = (f32[1024,1,128]{2,0,1:T(8,128)S(1)}, f32[1024,1,128]{2,0,1:T(8,128)S(1)}, u32[]{:S(2)}, u32[]{:S(2)}) collective-permute-start(f32[1024,1,128]{2,0,1:T(8,128)S(1)} %get-tuple-element.11), channel_id=1, source_target_pairs={{0,8},{8,16},{16,24},{24,32},{32,40},{40,48},{48,56},{56,64},{64,7... | collective-permute-start | bytes 1572872 | tf_op jit(solution)/shard_map/ppermute | solution.py:23
  19.9 17.0 %collective-permute-start.1 = (f32[1024,1,128]{2,0,1:T(8,128)S(1)}, f32[1024,1,128]{2,0,1:T(8,128)S(1)}, u32[]{:S(2)}, u32[]{:S(2)}) collective-permute-start(f32[1024,1,128]{2,0,1:T(8,128)S(1)} %get-tuple-element.10), channel_id=1, source_target_pairs={{8,0},{16,8},{24,16},{32,24},{40,32},{48,40},{56,48},{64,56},{72,6... | collective-permute-start | bytes 1572872 | tf_op jit(solution)/shard_map/ppermute | solution.py:24
  36.9 9.3 %copy-start = (f32[1024,18,128]{2,0,1:T(8,128)}, f32[1024,18,128]{2,0,1:T(8,128)S(1)}, u32[]{:S(2)}) copy-start(f32[1024,18,128]{2,0,1:T(8,128)S(1)} %constant_dynamic-update-slice_fusion) | copy-start | bytes 28311556
  51.8 10.2 %collective-permute-start.2 = (f32[1024,18,1]{0,2,1:T(1,128)S(1)}, f32[1024,18,1]{0,2,1:T(1,128)S(1)}, u32[]{:S(2)}, u32[]{:S(2)}) collective-permute-start(f32[1024,18,1]{0,2,1:T(1,128)S(1)} %copy.13), channel_id=1, source_target_pairs={{1,0},{2,1},{3,2},{4,3},{5,4},{6,5},{7,6},{9,8},{10,9},{11,10},{12... | collective-permute-start | bytes 221192 | tf_op jit(solution)/shard_map/ppermute | solution.py:24
  59.3 7.8 %collective-permute-start.3 = (f32[1024,18,1]{0,2,1:T(1,128)S(1)}, f32[1024,18,1]{0,2,1:T(1,128)S(1)}, u32[]{:S(2)}, u32[]{:S(2)}) collective-permute-start(f32[1024,18,1]{0,2,1:T(1,128)S(1)} %copy.15), channel_id=1, source_target_pairs={{0,1},{1,2},{2,3},{3,4},{4,5},{5,6},{6,7},{8,9},{9,10},{10,11},{11... | collective-permute-start | bytes 221192 | tf_op jit(solution)/shard_map/ppermute | solution.py:23
  98.7 234.1 %all-reduce.6.cloned.1.call-start = ((), (), s32[]{:S(2)}) async-start(), calls=%async_computation.1 | async-start | bytes 4194304 | tf_op jit(solution)/shard_map/psum | solution.py:70
Sparse Core Ops, SparseCore 0:
  98.8 73.6 all-reduce.3
  176.0 156.7 all-reduce.5
